TPU v7x, 32 devices: a whole 2x2x4 slice. The times are simulated.
32 devices in a mesh: table: 8 (over z, y), helper: 4 (over x, core).
Axes of the slice: x: 2, y: 2, z: 4, core: 2. Of those that a mesh axis runs over, the one named last changes fastest.
Arguments:
- tables: bfloat16 [64, 4096, 128], P('table'), may hold values from -6 to 6
- projections: bfloat16 [64, 128, 256], P('table'), may hold values from -0.0234375 to 0.0234375
- bag_rows: int32 [64, 8, 4, 8, 16], P('table', None, 'helper'), may hold values from 0 to 4095
- bag_lengths: int32 [64, 8, 4, 8], P('table', None, 'helper'), may hold values from 1 to 16
- candidates: bfloat16 [8, 4, 2048, 256], P('table', 'helper'), may hold values from -6 to 6
- request_counts: int32 [8, 4, 8], P('table', 'helper'), may hold values from 1 to 1024, as said below
- cross_down: bfloat16 [3, 512, 128], replicated, may hold values from -0.25 to 0.25
- cross_up: bfloat16 [3, 128, 512], replicated, may hold values from -0.5 to 0.5
- cross_bias: float32 [3, 512], replicated, may hold values from -3 to 3
- layer_one: bfloat16 [512, 1024], replicated, may hold values from -0.25 to 0.25
- bias_one: float32 [1024], replicated, may hold values from -2 to 2
- layer_two: bfloat16 [1024, 512], replicated, may hold values from -0.1875 to 0.1875
- bias_two: float32 [512], replicated, may hold values from -2 to 2
- layer_three: bfloat16 [512, 256], replicated, may hold values from -0.25 to 0.25
- bias_three: float32 [256], replicated, may hold values from -2 to 2
- score_weight: bfloat16 [256], replicated, may hold values from -0.375 to 0.375
Outputs:
- scores: float32 [8, 4, 2048], P('table', 'helper')
Inputs may be any that keep to these rules, and one draw needn't show every extreme that they name: For each (a, h) the 8 counts request_counts[a, h, :] sum to at most 2048; for every a exactly one h has a sum of exactly 2048, and in that list the first request holds exactly 1024 candidates.
All inputs are finite; a program needn't handle non-finite values.
Results may differ from a plain program's by a relative error of at most 0.018.
Values may be sent and summed in bfloat16 or wider, within the bound.
A program may use at most 128 MiB of HBM per device.

v0:
```python
import jax
import jax.numpy as jnp
from jax import lax
from jax.sharding import PartitionSpec as P

BLOCK = 256


def cross_network(features, context_rows, live_slots, weights):
    (
        cross_down,
        cross_up,
        cross_bias,
        layer_one,
        bias_one,
        layer_two,
        bias_two,
        layer_three,
        bias_three,
        score_weight,
    ) = weights
    cross_input = jnp.concatenate([features, context_rows], axis=1)
    anchor = cross_input.astype(jnp.float32)
    current = anchor
    for layer_number in range(cross_down.shape[0]):
        reduced = jnp.dot(
            current.astype(jnp.bfloat16),
            cross_down[layer_number],
            preferred_element_type=jnp.float32,
        ).astype(jnp.bfloat16)
        current = (
            anchor
            * (
                jnp.dot(reduced, cross_up[layer_number], preferred_element_type=jnp.float32)
                + cross_bias[layer_number]
            )
            + current
        )
    hidden = jax.nn.relu(
        jnp.dot(current.astype(jnp.bfloat16), layer_one, preferred_element_type=jnp.float32)
        + bias_one
    ).astype(jnp.bfloat16)
    hidden = jax.nn.relu(
        jnp.dot(hidden, layer_two, preferred_element_type=jnp.float32) + bias_two
    ).astype(jnp.bfloat16)
    hidden = jax.nn.relu(
        jnp.dot(hidden, layer_three, preferred_element_type=jnp.float32) + bias_three
    ).astype(jnp.bfloat16)
    result = jnp.dot(hidden, score_weight, preferred_element_type=jnp.float32)
    return jnp.where(live_slots, result, jnp.zeros_like(result))


def context_lookup(codes, context):
    labels = jnp.arange(context.shape[0], dtype=jnp.int32)
    choose = (codes[:, None] == labels[None, :]).astype(jnp.bfloat16)
    return jnp.dot(choose, context, preferred_element_type=jnp.float32).astype(jnp.bfloat16)


def block_scores(features, codes, context, weights):
    return cross_network(features, context_lookup(codes, context), codes >= 0, weights)


def slot_codes(counts, total_slots):
    ends = jnp.cumsum(counts)
    positions = jnp.arange(total_slots, dtype=jnp.int32)
    owner = jnp.sum((positions[:, None] >= ends[None, :]).astype(jnp.int32), axis=1)
    return jnp.where(owner < counts.shape[0], owner, -1)


def pool_table(table, indices, lengths):
    table_rows = table.shape[0]
    flat_rows = indices.reshape(-1, indices.shape[-1])
    flat_lengths = lengths.reshape(-1)
    labels = jnp.arange(table_rows, dtype=jnp.int32)
    tally = jnp.zeros((flat_rows.shape[0], table_rows), jnp.float32)
    for position in range(flat_rows.shape[1]):
        chosen = jnp.where(flat_lengths > position, flat_rows[:, position], -1)
        tally = tally + (chosen[:, None] == labels[None, :]).astype(jnp.float32)
    return jnp.dot(tally.astype(jnp.bfloat16), table, preferred_element_type=jnp.float32).astype(
        jnp.bfloat16
    )


def body(
    tables,
    projections,
    bag_rows,
    bag_lengths,
    candidates,
    request_counts,
    cross_down,
    cross_up,
    cross_bias,
    layer_one,
    bias_one,
    layer_two,
    bias_two,
    layer_three,
    bias_three,
    score_weight,
):
    weights = (
        cross_down,
        cross_up,
        cross_bias,
        layer_one,
        bias_one,
        layer_two,
        bias_two,
        layer_three,
        bias_three,
        score_weight,
    )
    local_tables = tables.shape[0]
    owners = bag_rows.shape[1]
    requests = bag_rows.shape[3]
    width = projections.shape[2]
    pooled_list = []
    for table_number in range(local_tables):
        pooled_list.append(
            pool_table(tables[table_number], bag_rows[table_number], bag_lengths[table_number])
        )
    projected = jnp.stack(
        [
            jnp.dot(
                pooled_list[table_number],
                projections[table_number],
                preferred_element_type=jnp.float32,
            ).astype(jnp.bfloat16)
            for table_number in range(local_tables)
        ],
        axis=0,
    )
    projected = projected.reshape(local_tables, owners, requests, width)
    received = lax.all_to_all(projected, "table", split_axis=1, concat_axis=0, tiled=True)
    context = jnp.sum(received.astype(jnp.float32), axis=(0, 1)).astype(jnp.bfloat16)
    features = candidates[0, 0]
    total_slots = features.shape[0]
    blocks = total_slots // BLOCK
    codes = slot_codes(request_counts[0, 0], total_slots)

    def empty_block():
        return jnp.zeros((BLOCK,), jnp.float32)

    def own_block(pieces):
        block_features, block_codes = pieces
        return lax.cond(
            block_codes[0] >= 0,
            lambda: block_scores(block_features, block_codes, context, weights),
            empty_block,
        )

    scores = lax.map(
        own_block, (features.reshape(blocks, BLOCK, width), codes.reshape(blocks, BLOCK))
    )
    result = scores.reshape(total_slots)
    return result.reshape(1, 1, total_slots)


def solution(mesh):
    in_specs = (
        P("table", None, None),
        P("table", None, None),
        P("table", None, "helper", None, None),
        P("table", None, "helper", None),
        P("table", "helper", None, None),
        P("table", "helper", None),
        P(),
        P(),
        P(),
        P(),
        P(),
        P(),
        P(),
        P(),
        P(),
        P(),
    )
    out_specs = P("table", "helper", None)
    return jax.shard_map(body, mesh=mesh, in_specs=in_specs, out_specs=out_specs, check_vma=False)
```

profile of v0, /device:TPU:2, one launch (start us, length us, event | category | flops | bytes accessed | tf_op | source)
XLA Modules:
  0.0 133.1 jit_solution(14103113073700829227)
XLA Ops:
  0.0 2.2 %compare_reduce_fusion.10 = (pred[8,8]{1,0:T(8,128)(4,1)S(1)}, pred[8,8]{1,0:T(8,128)(4,1)S(1)}, pred[8,8]{1,0:T(8,128)(4,1)S(1)}, pred[8,8]{1,0:T(8,128)(4,1)S(...) fusion(s32[8,8,1,8]{3,2,1,0:T(1,128)} %param.23), kind=kLoop, calls=%fused_computation.401 | loop fusion | flops 5760 | bytes 7808 | tf_op jit(solution)/shard_map/gt | solution.py:77
  2.2 1.3 compare_reduce_fusion.11
  3.6 0.9 slice_bitcast_fusion
  28.9 4.2 %fusion.46 = bf16[8,8,8,256]{3,2,0,1:T(8,128)(2,1)} fusion(bf16[8,4096,128]{2,1,0:T(8,128)(2,1)} %param.20, s32[64]{0:T(128)S(1)} %get-tuple-element.593, s32[64]{0:T(128)S(1)} %get-tuple-element.594, s32[64]{0:T(128)S(1)} %get-tuple-element.595, s32[64]{0:T(128)S(1)} %get-tuple-element.596, s32[64]{0:T(128)S(1)} %get-tuple-element.597, ...), kind=kOutput, calls=%fused_computation.61 | convolution fusion | flops 83910656 | bytes 1155072 | tf_op jit(solution)/shard_map/dot_general | solution.py:125
  33.2 4.4 %fusion.48 = bf16[8,8,8,256]{3,2,0,1:T(8,128)(2,1)} fusion(bf16[8,8,8,256]{3,2,0,1:T(8,128)(2,1)} %fusion.46, bf16[8,4096,128]{2,1,0:T(8,128)(2,1)} %param.20, s32[64]{0:T(128)S(1)} %get-tuple-element.609, s32[64]{0:T(128)S(1)} %get-tuple-element.610, s32[64]{0:T(128)S(1)} %get-tuple-element.611, s32[64]{0:T(128)S(1)} %get-tuple-element.612, ...), kind=kOutput, calls=%fused_computation.63 | convolution fusion | flops 83910656 | bytes 1155072 | tf_op jit(solution)/shard_map/dot_general | solution.py:125
  37.5 4.2 %fusion.50 = bf16[8,8,8,256]{3,2,0,1:T(8,128)(2,1)} fusion(bf16[8,8,8,256]{3,2,0,1:T(8,128)(2,1)} %fusion.48, bf16[8,4096,128]{2,1,0:T(8,128)(2,1)} %param.20, s32[64]{0:T(128)S(1)} %get-tuple-element.625, s32[64]{0:T(128)S(1)} %get-tuple-element.626, s32[64]{0:T(128)S(1)} %get-tuple-element.627, s32[64]{0:T(128)S(1)} %get-tuple-element.628, ...), kind=kOutput, calls=%fused_computation.65 | convolution fusion | flops 83910656 | bytes 1155072 | tf_op jit(solution)/shard_map/dot_general | solution.py:125
  41.8 4.2 %fusion.52 = bf16[8,8,8,256]{3,2,0,1:T(8,128)(2,1)} fusion(bf16[8,8,8,256]{3,2,0,1:T(8,128)(2,1)} %fusion.50, bf16[8,4096,128]{2,1,0:T(8,128)(2,1)} %param.20, s32[64]{0:T(128)S(1)} %get-tuple-element.641, s32[64]{0:T(128)S(1)} %get-tuple-element.642, s32[64]{0:T(128)S(1)} %get-tuple-element.643, s32[64]{0:T(128)S(1)} %get-tuple-element.644, ...), kind=kOutput, calls=%fused_computation.67 | convolution fusion | flops 83910656 | bytes 1155072 | tf_op jit(solution)/shard_map/dot_general | solution.py:125
  46.0 4.2 %fusion.54 = bf16[8,8,8,256]{3,2,0,1:T(8,128)(2,1)} fusion(bf16[8,8,8,256]{3,2,0,1:T(8,128)(2,1)} %fusion.52, bf16[8,4096,128]{2,1,0:T(8,128)(2,1)} %param.20, s32[64]{0:T(128)S(1)} %get-tuple-element.657, s32[64]{0:T(128)S(1)} %get-tuple-element.658, s32[64]{0:T(128)S(1)} %get-tuple-element.659, s32[64]{0:T(128)S(1)} %get-tuple-element.660, ...), kind=kOutput, calls=%fused_computation.69 | convolution fusion | flops 83910656 | bytes 1155072 | tf_op jit(solution)/shard_map/dot_general | solution.py:125
  50.2 4.2 %fusion.56 = bf16[8,8,8,256]{3,2,0,1:T(8,128)(2,1)} fusion(bf16[8,8,8,256]{3,2,0,1:T(8,128)(2,1)} %fusion.54, bf16[8,4096,128]{2,1,0:T(8,128)(2,1)} %param.20, s32[64]{0:T(128)S(1)} %get-tuple-element.673, s32[64]{0:T(128)S(1)} %get-tuple-element.674, s32[64]{0:T(128)S(1)} %get-tuple-element.675, s32[64]{0:T(128)S(1)} %get-tuple-element.676, ...), kind=kOutput, calls=%fused_computation.71 | convolution fusion | flops 83910656 | bytes 1155072 | tf_op jit(solution)/shard_map/dot_general | solution.py:125
  54.4 4.3 %fusion.58 = bf16[8,8,8,256]{3,2,0,1:T(8,128)(2,1)} fusion(bf16[8,8,8,256]{3,2,0,1:T(8,128)(2,1)} %fusion.56, bf16[8,4096,128]{2,1,0:T(8,128)(2,1)} %param.20, s32[64]{0:T(128)S(1)} %get-tuple-element.689, s32[64]{0:T(128)S(1)} %get-tuple-element.690, s32[64]{0:T(128)S(1)} %get-tuple-element.691, s32[64]{0:T(128)S(1)} %get-tuple-element.692, ...), kind=kOutput, calls=%fused_computation.73 | convolution fusion | flops 83910656 | bytes 1155072 | tf_op jit(solution)/shard_map/dot_general | solution.py:125
  58.7 4.5 %fusion.60 = bf16[8,8,8,256]{3,2,0,1:T(8,128)(2,1)} fusion(bf16[8,8,8,256]{3,2,0,1:T(8,128)(2,1)} %fusion.58, bf16[8,4096,128]{2,1,0:T(8,128)(2,1)} %param.20, s32[64]{0:T(128)S(1)} %get-tuple-element.705, s32[64]{0:T(128)S(1)} %get-tuple-element.706, s32[64]{0:T(128)S(1)} %get-tuple-element.707, s32[64]{0:T(128)S(1)} %get-tuple-element.708, ...), kind=kOutput, calls=%fused_computation.75 | convolution fusion | flops 83910656 | bytes 1155072 | tf_op jit(solution)/shard_map/dot_general | solution.py:125
  63.2 5.8 %all-to-all-start = ((bf16[8,8,8,256]{3,2,0,1:T(8,128)(2,1)}), bf16[8,8,8,256]{3,2,0,1:T(8,128)(2,1)S(1)}, u32[]{:S(2)}, u32[]{:S(2)}) async-start(bf16[8,8,8,256]{3,2,0,1:T(8,128)(2,1)} %fusion.60), calls=%async_computation | async-start | bytes 524288 | tf_op jit(solution)/shard_map/all_to_all | solution.py:135
  69.1 0.5 copy.437
  69.9 8.1 %all-to-all-done = bf16[8,8,8,256]{3,2,0,1:T(8,128)(2,1)S(1)} async-done(((bf16[8,8,8,256]{3,2,0,1:T(8,128)(2,1)}), bf16[8,8,8,256]{3,2,0,1:T(8,128)(2,1)S(1)}, u32[]{:S(2)}, u32[]{:S(2)}) %all-to-all-start) | async-done | bytes 262176 | tf_op jit(solution)/shard_map/all_to_all | solution.py:135
  78.1 54.4 %while.10 = (s32[]{:T(128)}, f32[8,256]{1,0:T(8,128)S(1)}, s32[8,256]{1,0:T(8,128)S(1)}, bf16[8,256,256]{1,2,0:T(8,128)(2,1)S(1)}, bf16[8,256]{1,0:T(8,128)(2,1)...) while((s32[]{:T(128)}, f32[8,256]{1,0:T(8,128)S(1)}, ...), condition=%wide.region_6.7_spmd, body=%wide.region_3.6_spmd.sunk | while | flops 811698688 | bytes 8822575 | solution.py:153
  78.1 0.6 fusion.383
  79.4 5.4 %conditional.2 = (f32[1,256]{1,0:T(1,128)S(1)}) conditional(s32[]{:T(128)} %bitcast.417, () %tuple.437, (s32[1,256]{1,0:T(1,128)S(1)}, bf16[8,256,256]{1,2,0:T(8,128)(2,1)S(1)}, s32[]{:T(128)}, bf16[8,256]{1,0:T(8,128)(2,1)S(1)}, bf16[3,512,128]{2,1,0:T(8,128)(2,1)S(1)}, /*index=5*/bf16[3,128,512]{2,1,0:T(8,128)(2,1)S(1)}, f32[3,512]{1,0:T(4,128)S(1)}, ...), branch_computations={%region_4.4_spmd, %region_5.5_spmd} | conditional | flops 811698688 | bytes 8818188 | solution.py:147
  79.8 0.5 fusion.4
  80.3 0.5 fusion.6
  81.3 2.3 %fusion.10 = bf16[256,512]{1,0:T(8,128)(2,1)S(1)} fusion(bf16[1024,512]{1,0:T(8,128)(2,1)} %get-tuple-element.138, bf16[256,512]{0,1:T(8,128)(2,1)S(1)} %fusion.9, bf16[512,1024]{1,0:T(8,128)(2,1)} %get-tuple-element.136, f32[1024]{0:T(1024)S(1)} %get-tuple-element.137, f32[512]{0:T(512)S(1)} %get-tuple-element.139), kind=kOutput, calls=%fused_computation.15 | convolution fusion | flops 538050560 | bytes 2627584 | tf_op jit(solution)/shard_map/while/body/eval_jaxpr/cond/branch_1_fun/dot_general | solution.py:44
  83.6 1.3 fusion.13
  84.9 0.6 fusion.383
  86.2 5.4 %conditional.2 = (f32[1,256]{1,0:T(1,128)S(1)}) conditional(s32[]{:T(128)} %bitcast.417, () %tuple.437, (s32[1,256]{1,0:T(1,128)S(1)}, bf16[8,256,256]{1,2,0:T(8,128)(2,1)S(1)}, s32[]{:T(128)}, bf16[8,256]{1,0:T(8,128)(2,1)S(1)}, bf16[3,512,128]{2,1,0:T(8,128)(2,1)S(1)}, /*index=5*/bf16[3,128,512]{2,1,0:T(8,128)(2,1)S(1)}, f32[3,512]{1,0:T(4,128)S(1)}, ...), branch_computations={%region_4.4_spmd, %region_5.5_spmd} | conditional | flops 811698688 | bytes 8818188 | solution.py:147
  86.6 0.5 fusion.4
  87.1 0.5 fusion.6
  88.1 2.3 %fusion.10 = bf16[256,512]{1,0:T(8,128)(2,1)S(1)} fusion(bf16[1024,512]{1,0:T(8,128)(2,1)} %get-tuple-element.138, bf16[256,512]{0,1:T(8,128)(2,1)S(1)} %fusion.9, bf16[512,1024]{1,0:T(8,128)(2,1)} %get-tuple-element.136, f32[1024]{0:T(1024)S(1)} %get-tuple-element.137, f32[512]{0:T(512)S(1)} %get-tuple-element.139), kind=kOutput, calls=%fused_computation.15 | convolution fusion | flops 538050560 | bytes 2627584 | tf_op jit(solution)/shard_map/while/body/eval_jaxpr/cond/branch_1_fun/dot_general | solution.py:44
  90.4 1.3 fusion.13
  91.7 0.6 fusion.383
  93.0 5.4 %conditional.2 = (f32[1,256]{1,0:T(1,128)S(1)}) conditional(s32[]{:T(128)} %bitcast.417, () %tuple.437, (s32[1,256]{1,0:T(1,128)S(1)}, bf16[8,256,256]{1,2,0:T(8,128)(2,1)S(1)}, s32[]{:T(128)}, bf16[8,256]{1,0:T(8,128)(2,1)S(1)}, bf16[3,512,128]{2,1,0:T(8,128)(2,1)S(1)}, /*index=5*/bf16[3,128,512]{2,1,0:T(8,128)(2,1)S(1)}, f32[3,512]{1,0:T(4,128)S(1)}, ...), branch_computations={%region_4.4_spmd, %region_5.5_spmd} | conditional | flops 811698688 | bytes 8818188 | solution.py:147
  93.4 0.5 fusion.4
  93.9 0.5 fusion.6
  94.9 2.3 %fusion.10 = bf16[256,512]{1,0:T(8,128)(2,1)S(1)} fusion(bf16[1024,512]{1,0:T(8,128)(2,1)} %get-tuple-element.138, bf16[256,512]{0,1:T(8,128)(2,1)S(1)} %fusion.9, bf16[512,1024]{1,0:T(8,128)(2,1)} %get-tuple-element.136, f32[1024]{0:T(1024)S(1)} %get-tuple-element.137, f32[512]{0:T(512)S(1)} %get-tuple-element.139), kind=kOutput, calls=%fused_computation.15 | convolution fusion | flops 538050560 | bytes 2627584 | tf_op jit(solution)/shard_map/while/body/eval_jaxpr/cond/branch_1_fun/dot_general | solution.py:44
  97.2 1.3 fusion.13
  98.5 0.6 fusion.383
  99.8 5.4 %conditional.2 = (f32[1,256]{1,0:T(1,128)S(1)}) conditional(s32[]{:T(128)} %bitcast.417, () %tuple.437, (s32[1,256]{1,0:T(1,128)S(1)}, bf16[8,256,256]{1,2,0:T(8,128)(2,1)S(1)}, s32[]{:T(128)}, bf16[8,256]{1,0:T(8,128)(2,1)S(1)}, bf16[3,512,128]{2,1,0:T(8,128)(2,1)S(1)}, /*index=5*/bf16[3,128,512]{2,1,0:T(8,128)(2,1)S(1)}, f32[3,512]{1,0:T(4,128)S(1)}, ...), branch_computations={%region_4.4_spmd, %region_5.5_spmd} | conditional | flops 811698688 | bytes 8818188 | solution.py:147
  100.2 0.5 fusion.4
  100.7 0.5 fusion.6
  101.7 2.3 %fusion.10 = bf16[256,512]{1,0:T(8,128)(2,1)S(1)} fusion(bf16[1024,512]{1,0:T(8,128)(2,1)} %get-tuple-element.138, bf16[256,512]{0,1:T(8,128)(2,1)S(1)} %fusion.9, bf16[512,1024]{1,0:T(8,128)(2,1)} %get-tuple-element.136, f32[1024]{0:T(1024)S(1)} %get-tuple-element.137, f32[512]{0:T(512)S(1)} %get-tuple-element.139), kind=kOutput, calls=%fused_computation.15 | convolution fusion | flops 538050560 | bytes 2627584 | tf_op jit(solution)/shard_map/while/body/eval_jaxpr/cond/branch_1_fun/dot_general | solution.py:44
  104.0 1.3 fusion.13
  105.3 0.6 fusion.383
  106.6 5.4 %conditional.2 = (f32[1,256]{1,0:T(1,128)S(1)}) conditional(s32[]{:T(128)} %bitcast.417, () %tuple.437, (s32[1,256]{1,0:T(1,128)S(1)}, bf16[8,256,256]{1,2,0:T(8,128)(2,1)S(1)}, s32[]{:T(128)}, bf16[8,256]{1,0:T(8,128)(2,1)S(1)}, bf16[3,512,128]{2,1,0:T(8,128)(2,1)S(1)}, /*index=5*/bf16[3,128,512]{2,1,0:T(8,128)(2,1)S(1)}, f32[3,512]{1,0:T(4,128)S(1)}, ...), branch_computations={%region_4.4_spmd, %region_5.5_spmd} | conditional | flops 811698688 | bytes 8818188 | solution.py:147
  107.0 0.5 fusion.4
  107.5 0.5 fusion.6
  108.4 2.3 %fusion.10 = bf16[256,512]{1,0:T(8,128)(2,1)S(1)} fusion(bf16[1024,512]{1,0:T(8,128)(2,1)} %get-tuple-element.138, bf16[256,512]{0,1:T(8,128)(2,1)S(1)} %fusion.9, bf16[512,1024]{1,0:T(8,128)(2,1)} %get-tuple-element.136, f32[1024]{0:T(1024)S(1)} %get-tuple-element.137, f32[512]{0:T(512)S(1)} %get-tuple-element.139), kind=kOutput, calls=%fused_computation.15 | convolution fusion | flops 538050560 | bytes 2627584 | tf_op jit(solution)/shard_map/while/body/eval_jaxpr/cond/branch_1_fun/dot_general | solution.py:44
  110.7 1.3 fusion.13
  112.1 0.6 fusion.383
  113.4 5.4 %conditional.2 = (f32[1,256]{1,0:T(1,128)S(1)}) conditional(s32[]{:T(128)} %bitcast.417, () %tuple.437, (s32[1,256]{1,0:T(1,128)S(1)}, bf16[8,256,256]{1,2,0:T(8,128)(2,1)S(1)}, s32[]{:T(128)}, bf16[8,256]{1,0:T(8,128)(2,1)S(1)}, bf16[3,512,128]{2,1,0:T(8,128)(2,1)S(1)}, /*index=5*/bf16[3,128,512]{2,1,0:T(8,128)(2,1)S(1)}, f32[3,512]{1,0:T(4,128)S(1)}, ...), branch_computations={%region_4.4_spmd, %region_5.5_spmd} | conditional | flops 811698688 | bytes 8818188 | solution.py:147
  113.8 0.5 fusion.4
  114.2 0.5 fusion.6
  115.2 2.3 %fusion.10 = bf16[256,512]{1,0:T(8,128)(2,1)S(1)} fusion(bf16[1024,512]{1,0:T(8,128)(2,1)} %get-tuple-element.138, bf16[256,512]{0,1:T(8,128)(2,1)S(1)} %fusion.9, bf16[512,1024]{1,0:T(8,128)(2,1)} %get-tuple-element.136, f32[1024]{0:T(1024)S(1)} %get-tuple-element.137, f32[512]{0:T(512)S(1)} %get-tuple-element.139), kind=kOutput, calls=%fused_computation.15 | convolution fusion | flops 538050560 | bytes 2627584 | tf_op jit(solution)/shard_map/while/body/eval_jaxpr/cond/branch_1_fun/dot_general | solution.py:44
  117.5 1.3 fusion.13
  118.9 0.6 fusion.383
  120.2 5.4 %conditional.2 = (f32[1,256]{1,0:T(1,128)S(1)}) conditional(s32[]{:T(128)} %bitcast.417, () %tuple.437, (s32[1,256]{1,0:T(1,128)S(1)}, bf16[8,256,256]{1,2,0:T(8,128)(2,1)S(1)}, s32[]{:T(128)}, bf16[8,256]{1,0:T(8,128)(2,1)S(1)}, bf16[3,512,128]{2,1,0:T(8,128)(2,1)S(1)}, /*index=5*/bf16[3,128,512]{2,1,0:T(8,128)(2,1)S(1)}, f32[3,512]{1,0:T(4,128)S(1)}, ...), branch_computations={%region_4.4_spmd, %region_5.5_spmd} | conditional | flops 811698688 | bytes 8818188 | solution.py:147
  120.5 0.5 fusion.4
  121.0 0.5 fusion.6
  122.0 2.3 %fusion.10 = bf16[256,512]{1,0:T(8,128)(2,1)S(1)} fusion(bf16[1024,512]{1,0:T(8,128)(2,1)} %get-tuple-element.138, bf16[256,512]{0,1:T(8,128)(2,1)S(1)} %fusion.9, bf16[512,1024]{1,0:T(8,128)(2,1)} %get-tuple-element.136, f32[1024]{0:T(1024)S(1)} %get-tuple-element.137, f32[512]{0:T(512)S(1)} %get-tuple-element.139), kind=kOutput, calls=%fused_computation.15 | convolution fusion | flops 538050560 | bytes 2627584 | tf_op jit(solution)/shard_map/while/body/eval_jaxpr/cond/branch_1_fun/dot_general | solution.py:44
  124.3 1.3 fusion.13
  125.7 0.6 fusion.383
  127.0 5.4 %conditional.2 = (f32[1,256]{1,0:T(1,128)S(1)}) conditional(s32[]{:T(128)} %bitcast.417, () %tuple.437, (s32[1,256]{1,0:T(1,128)S(1)}, bf16[8,256,256]{1,2,0:T(8,128)(2,1)S(1)}, s32[]{:T(128)}, bf16[8,256]{1,0:T(8,128)(2,1)S(1)}, bf16[3,512,128]{2,1,0:T(8,128)(2,1)S(1)}, /*index=5*/bf16[3,128,512]{2,1,0:T(8,128)(2,1)S(1)}, f32[3,512]{1,0:T(4,128)S(1)}, ...), branch_computations={%region_4.4_spmd, %region_5.5_spmd} | conditional | flops 811698688 | bytes 8818188 | solution.py:147
  127.3 0.5 fusion.4
  127.8 0.5 fusion.6
  128.8 2.3 %fusion.10 = bf16[256,512]{1,0:T(8,128)(2,1)S(1)} fusion(bf16[1024,512]{1,0:T(8,128)(2,1)} %get-tuple-element.138, bf16[256,512]{0,1:T(8,128)(2,1)S(1)} %fusion.9, bf16[512,1024]{1,0:T(8,128)(2,1)} %get-tuple-element.136, f32[1024]{0:T(1024)S(1)} %get-tuple-element.137, f32[512]{0:T(512)S(1)} %get-tuple-element.139), kind=kOutput, calls=%fused_computation.15 | convolution fusion | flops 538050560 | bytes 2627584 | tf_op jit(solution)/shard_map/while/body/eval_jaxpr/cond/branch_1_fun/dot_general | solution.py:44
  131.1 1.3 fusion.13
  132.5 0.6 reshape_reshape.3
  (418 shorter events, 30.8 us)
Async XLA Ops:
  0.0 28.9 %copy-start.4 = (bf16[8,128,256]{2,1,0:T(8,128)(2,1)S(1)}, bf16[8,128,256]{2,1,0:T(8,128)(2,1)}, u32[]{:S(2)}) copy-start(bf16[8,128,256]{2,1,0:T(8,128)(2,1)} %param.21) | copy-start | bytes 1572868
  54.4 14.7 %copy-start.2 = (bf16[1,1,2048,256]{3,2,1,0:T(8,128)(2,1)S(1)}, bf16[1,1,2048,256]{3,2,1,0:T(8,128)(2,1)}, u32[]{:S(2)}) copy-start(bf16[1,1,2048,256]{3,2,1,0:T(8,128)(2,1)} %param.24) | copy-start | bytes 3145732
  54.4 15.2 %copy-start.8 = (s32[1,1,8]{2,1,0:T(1,128)S(1)}, s32[1,1,8]{2,1,0:T(1,128)}, u32[]{:S(2)}) copy-start(s32[1,1,8]{2,1,0:T(1,128)} %param.25) | copy-start | bytes 100
  58.7 19.4 %copy-start = (bf16[3,512,128]{2,1,0:T(8,128)(2,1)S(1)}, bf16[3,512,128]{2,1,0:T(8,128)(2,1)}, u32[]{:S(2)}) copy-start(bf16[3,512,128]{2,1,0:T(8,128)(2,1)} %param.26) | copy-start | bytes 1179652
  58.7 19.4 %copy-start.1 = (bf16[3,128,512]{2,1,0:T(8,128)(2,1)S(1)}, bf16[3,128,512]{2,1,0:T(8,128)(2,1)}, u32[]{:S(2)}) copy-start(bf16[3,128,512]{2,1,0:T(8,128)(2,1)} %param.27) | copy-start | bytes 1179652
  58.7 19.4 %copy-start.3 = (f32[3,512]{1,0:T(4,128)S(1)}, f32[3,512]{1,0:T(4,128)}, u32[]{:S(2)}) copy-start(f32[3,512]{1,0:T(4,128)} %param.28) | copy-start | bytes 18436
  58.7 19.4 %copy-start.5 = (f32[1024]{0:T(1024)S(1)}, f32[1024]{0:T(1024)}, u32[]{:S(2)}) copy-start(f32[1024]{0:T(1024)} %param.30) | copy-start | bytes 12292
  58.7 19.4 %copy-start.6 = (f32[512]{0:T(512)S(1)}, f32[512]{0:T(512)}, u32[]{:S(2)}) copy-start(f32[512]{0:T(512)} %param.32) | copy-start | bytes 6148
  58.7 19.4 %copy-start.7 = (f32[256]{0:T(256)S(1)}, f32[256]{0:T(256)}, u32[]{:S(2)}) copy-start(f32[256]{0:T(256)} %param.34) | copy-start | bytes 3076
  58.7 19.4 %copy-start.9 = (bf16[256]{0:T(256)(128)(2,1)S(1)}, bf16[256]{0:T(256)(128)(2,1)}, u32[]{:S(2)}) copy-start(bf16[256]{0:T(256)(128)(2,1)} %param.35) | copy-start | bytes 1540
  63.2 14.8 %all-to-all-start = ((bf16[8,8,8,256]{3,2,0,1:T(8,128)(2,1)}), bf16[8,8,8,256]{3,2,0,1:T(8,128)(2,1)S(1)}, u32[]{:S(2)}, u32[]{:S(2)}) async-start(bf16[8,8,8,256]{3,2,0,1:T(8,128)(2,1)} %fusion.60), calls=%async_computation | async-start | bytes 524288 | tf_op jit(solution)/shard_map/all_to_all | solution.py:135
where the time goes:
time: 134 us; the launch traced here: 133 us
  matrix products  76.8 us (57%)
  local copies, waits for them, and re-layouts  26 us (19%)
  other arithmetic  9.15 us (7%)
  waiting for transfers between devices  8.07 us (6%)
  loops' own time  6.45 us (5%)
  starting transfers between devices  5.83 us (4%)
    dot_general x8, matrix products, body(): jnp.dot(pooled_list[table_number], projections[table_number], preferred_e...  34.2 us
    dot_general x8, matrix products, cross_network(): jnp.dot(hidden, layer_two, preferred_element_type=jnp.float32) + bias_two  18.3 us
    gt x128, local copies, waits for them, and re-layouts, pool_table(): chosen = jnp.where(flat_lengths > position, flat_rows[:, position], -1)  12.5 us
    dot_general x24, matrix products, cross_network(): jnp.dot(reduced, cross_up[layer_number], preferred_element_type=jnp.float32)  11.7 us
    dot_general x8, matrix products, cross_network(): result = jnp.dot(hidden, score_weight, preferred_element_type=jnp.float32)  10.4 us
    unnamed x148, local copies, waits for them, and re-layouts  9.31 us
    all_to_all x1, waiting for transfers between devices, body(): lax.all_to_all(projected, 'table', split_axis=1, concat_axis=0, tiled=True)  8.07 us
    all_to_all x1, starting transfers between devices, body(): lax.all_to_all(projected, 'table', split_axis=1, concat_axis=0, tiled=True)  5.83 us
  transfers between devices with their start and end apart: 1, of which 1 were waited for; matrix products, arithmetic and copies ran while one was open for 1% of the time, Pallas kernels for 0%

commit v1 on v0

--- a/solution.py
+++ b/solution.py
@@ -132,7 +132,9 @@
         axis=0,
     )
     projected = projected.reshape(local_tables, owners, requests, width)
-    received = lax.all_to_all(projected, "table", split_axis=1, concat_axis=0, tiled=True)
+    cells = jnp.split(projected, lax.axis_size("table"), axis=1)
+    incoming = lax.all_to_all(jnp.stack(cells), "table", 0, 0)
+    received = jnp.concatenate(incoming, axis=0)
     context = jnp.sum(received.astype(jnp.float32), axis=(0, 1)).astype(jnp.bfloat16)
     features = candidates[0, 0]
     total_slots = features.shape[0]

time: 134 us -> 126 us (0.940)
  matrix products: 76.8 us -> 64.2 us
  local copies, waits for them, and re-layouts: 26 us -> 30.9 us
    dot_general x8, matrix products: 10.4 us -> 2.78 us  [cross_network(): result = jnp.dot(hidden, score_weight, preferred_element_type=jnp.float32)]
    dot_general x8, matrix products: 34.2 us -> 29.2 us  [body(): jnp.dot(pooled_list[table_number], projections[table_number], preferred_e...]
    unnamed x148 -> x157, local copies, waits for them, and re-layouts: 9.31 us -> 13.6 us
where the time goes in v1:
time: 126 us; the launch traced here: 125 us
  matrix products  64.2 us (51%)
  local copies, waits for them, and re-layouts  30.9 us (25%)
  other arithmetic  9.15 us (7%)
  waiting for transfers between devices  8.07 us (6%)
  loops' own time  6.45 us (5%)
  starting transfers between devices  5.83 us (5%)
    dot_general x8, matrix products, body(): jnp.dot(pooled_list[table_number], projections[table_number], preferred_e...  29.2 us
    dot_general x8, matrix products, cross_network(): jnp.dot(hidden, layer_two, preferred_element_type=jnp.float32) + bias_two  18.3 us
    unnamed x157, local copies, waits for them, and re-layouts  13.6 us
    gt x128, local copies, waits for them, and re-layouts, pool_table(): chosen = jnp.where(flat_lengths > position, flat_rows[:, position], -1)  12.5 us
    dot_general x24, matrix products, cross_network(): jnp.dot(reduced, cross_up[layer_number], preferred_element_type=jnp.float32)  11.7 us
    all_to_all x1, waiting for transfers between devices, body(): incoming = lax.all_to_all(jnp.stack(cells), 'table', 0, 0)  8.07 us
    all_to_all x1, starting transfers between devices, body(): incoming = lax.all_to_all(jnp.stack(cells), 'table', 0, 0)  5.83 us
    another operation x1, loops' own time, body(): lax.map(own_block, (features.reshape(blocks, BLOCK, width), codes.reshape...  5.8 us
  transfers between devices with their start and end apart: 1, of which 1 were waited for; matrix products, arithmetic and copies ran while one was open for 1% of the time, Pallas kernels for 0%

profile of v1, /device:TPU:2, one launch (start us, length us, event | category | flops | bytes accessed | tf_op | source)
XLA Modules:
  0.0 125.4 jit_solution(4641504969581677895)
XLA Ops:
  0.0 2.2 %compare_reduce_fusion.10 = (pred[8,8]{1,0:T(8,128)(4,1)S(1)}, pred[8,8]{1,0:T(8,128)(4,1)S(1)}, pred[8,8]{1,0:T(8,128)(4,1)S(1)}, pred[8,8]{1,0:T(8,128)(4,1)S(...) fusion(s32[8,8,1,8]{3,2,1,0:T(1,128)} %param.23), kind=kLoop, calls=%fused_computation.417 | loop fusion | flops 5760 | bytes 7808 | tf_op jit(solution)/shard_map/gt | solution.py:77
  2.2 1.3 %compare_reduce_fusion.11 = (pred[8,8]{1,0:T(8,128)(4,1)S(1)}, pred[8,8]{1,0:T(8,128)(4,1)S(1)}, pred[8,8]{1,0:T(8,128)(4,1)S(1)}, pred[8,8]{1,0:T(8,128)(4,1)S(...) fusion(s32[8,8,1,8]{3,2,1,0:T(1,128)} %param.23), kind=kLoop, calls=%fused_computation.418 | loop fusion | flops 2432 | bytes 3712 | tf_op jit(solution)/shard_map/gt | solution.py:77
  3.6 0.9 slice_bitcast_fusion.8
  28.9 3.6 %fusion.46 = bf16[8,8,8,256]{3,2,1,0:T(8,128)(2,1)S(1)} fusion(bf16[8,4096,128]{2,1,0:T(8,128)(2,1)} %param.20, s32[64]{0:T(128)S(1)} %get-tuple-element.578, s32[64]{0:T(128)S(1)} %get-tuple-element.579, s32[64]{0:T(128)S(1)} %get-tuple-element.580, s32[64]{0:T(128)S(1)} %get-tuple-element.581, s32[64]{0:T(128)S(1)} %get-tuple-element.582, ...), kind=kOutput, calls=%fused_computation.61 | convolution fusion | flops 83910656 | bytes 1155072 | tf_op jit(solution)/shard_map/dot_general | solution.py:125
  32.5 3.8 %fusion.48 = bf16[8,8,8,256]{3,2,1,0:T(8,128)(2,1)S(1)} fusion(bf16[8,8,8,256]{3,2,1,0:T(8,128)(2,1)S(1)} %fusion.46, bf16[8,4096,128]{2,1,0:T(8,128)(2,1)} %param.20, s32[64]{0:T(128)S(1)} %get-tuple-element.594, s32[64]{0:T(128)S(1)} %get-tuple-element.595, s32[64]{0:T(128)S(1)} %get-tuple-element.596, s32[64]{0:T(128)S(1)} %get-tuple-element.597, ...), kind=kOutput, calls=%fused_computation.63 | convolution fusion | flops 83910656 | bytes 1155072 | tf_op jit(solution)/shard_map/dot_general | solution.py:125
  36.3 3.6 %fusion.50 = bf16[8,8,8,256]{3,2,1,0:T(8,128)(2,1)S(1)} fusion(bf16[8,8,8,256]{3,2,1,0:T(8,128)(2,1)S(1)} %fusion.48, bf16[8,4096,128]{2,1,0:T(8,128)(2,1)} %param.20, s32[64]{0:T(128)S(1)} %get-tuple-element.610, s32[64]{0:T(128)S(1)} %get-tuple-element.611, s32[64]{0:T(128)S(1)} %get-tuple-element.612, s32[64]{0:T(128)S(1)} %get-tuple-element.613, ...), kind=kOutput, calls=%fused_computation.65 | convolution fusion | flops 83910656 | bytes 1155072 | tf_op jit(solution)/shard_map/dot_general | solution.py:125
  39.8 3.6 %fusion.52 = bf16[8,8,8,256]{3,2,1,0:T(8,128)(2,1)S(1)} fusion(bf16[8,8,8,256]{3,2,1,0:T(8,128)(2,1)S(1)} %fusion.50, bf16[8,4096,128]{2,1,0:T(8,128)(2,1)} %param.20, s32[64]{0:T(128)S(1)} %get-tuple-element.626, s32[64]{0:T(128)S(1)} %get-tuple-element.627, s32[64]{0:T(128)S(1)} %get-tuple-element.628, s32[64]{0:T(128)S(1)} %get-tuple-element.629, ...), kind=kOutput, calls=%fused_computation.67 | convolution fusion | flops 83910656 | bytes 1155072 | tf_op jit(solution)/shard_map/dot_general | solution.py:125
  43.4 3.6 %fusion.54 = bf16[8,8,8,256]{3,2,1,0:T(8,128)(2,1)S(1)} fusion(bf16[8,8,8,256]{3,2,1,0:T(8,128)(2,1)S(1)} %fusion.52, bf16[8,4096,128]{2,1,0:T(8,128)(2,1)} %param.20, s32[64]{0:T(128)S(1)} %get-tuple-element.642, s32[64]{0:T(128)S(1)} %get-tuple-element.643, s32[64]{0:T(128)S(1)} %get-tuple-element.644, s32[64]{0:T(128)S(1)} %get-tuple-element.645, ...), kind=kOutput, calls=%fused_computation.69 | convolution fusion | flops 83910656 | bytes 1155072 | tf_op jit(solution)/shard_map/dot_general | solution.py:125
  47.0 3.6 %fusion.56 = bf16[8,8,8,256]{3,2,1,0:T(8,128)(2,1)S(1)} fusion(bf16[8,8,8,256]{3,2,1,0:T(8,128)(2,1)S(1)} %fusion.54, bf16[8,4096,128]{2,1,0:T(8,128)(2,1)} %param.20, s32[64]{0:T(128)S(1)} %get-tuple-element.658, s32[64]{0:T(128)S(1)} %get-tuple-element.659, s32[64]{0:T(128)S(1)} %get-tuple-element.660, s32[64]{0:T(128)S(1)} %get-tuple-element.661, ...), kind=kOutput, calls=%fused_computation.71 | convolution fusion | flops 83910656 | bytes 1155072 | tf_op jit(solution)/shard_map/dot_general | solution.py:125
  50.6 3.7 %fusion.58 = bf16[8,8,8,256]{3,2,1,0:T(8,128)(2,1)S(1)} fusion(bf16[8,8,8,256]{3,2,1,0:T(8,128)(2,1)S(1)} %fusion.56, bf16[8,4096,128]{2,1,0:T(8,128)(2,1)} %param.20, s32[64]{0:T(128)S(1)} %get-tuple-element.674, s32[64]{0:T(128)S(1)} %get-tuple-element.675, s32[64]{0:T(128)S(1)} %get-tuple-element.676, s32[64]{0:T(128)S(1)} %get-tuple-element.677, ...), kind=kOutput, calls=%fused_computation.73 | convolution fusion | flops 83910656 | bytes 1155072 | tf_op jit(solution)/shard_map/dot_general | solution.py:125
  54.4 3.9 %fusion.60 = bf16[8,8,8,256]{3,2,1,0:T(8,128)(2,1)S(1)} fusion(bf16[8,8,8,256]{3,2,1,0:T(8,128)(2,1)S(1)} %fusion.58, bf16[8,4096,128]{2,1,0:T(8,128)(2,1)} %param.20, s32[64]{0:T(128)S(1)} %get-tuple-element.690, s32[64]{0:T(128)S(1)} %get-tuple-element.691, s32[64]{0:T(128)S(1)} %get-tuple-element.692, s32[64]{0:T(128)S(1)} %get-tuple-element.693, ...), kind=kOutput, calls=%fused_computation.75 | convolution fusion | flops 83910656 | bytes 1155072 | tf_op jit(solution)/shard_map/dot_general | solution.py:125
  58.3 0.6 constant_dynamic-update-slice_fusion.7
  58.9 0.6 constant_dynamic-update-slice_fusion.6
  59.5 0.6 constant_dynamic-update-slice_fusion.5
  60.1 0.6 constant_dynamic-update-slice_fusion.4
  60.7 0.6 constant_dynamic-update-slice_fusion.3
  61.3 0.6 constant_dynamic-update-slice_fusion.2
  61.9 0.6 constant_dynamic-update-slice_fusion.1
  62.5 0.6 constant_dynamic-update-slice_fusion
  63.1 5.8 %all-to-all-start = ((bf16[8,8,1,8,256]{4,3,1,2,0:T(8,128)(2,1)}), bf16[8,8,1,8,256]{4,3,1,2,0:T(8,128)(2,1)S(1)}, u32[]{:S(2)}, u32[]{:S(2)}) async-start(bf16[8,8,1,8,256]{4,3,1,2,0:T(8,128)(2,1)} %constant_dynamic-update-slice_fusion), calls=%async_computation | async-start | bytes 524288 | tf_op jit(solution)/shard_map/all_to_all | solution.py:136
  69.0 0.5 copy.310
  69.8 8.1 %all-to-all-done = bf16[8,8,1,8,256]{4,3,1,2,0:T(8,128)(2,1)S(1)} async-done(((bf16[8,8,1,8,256]{4,3,1,2,0:T(8,128)(2,1)}), bf16[8,8,1,8,256]{4,3,1,2,0:T(8,128)(2,1)S(1)}, u32[]{:S(2)}, u32[]{:S(2)}) %all-to-all-start) | async-done | bytes 262176 | tf_op jit(solution)/shard_map/all_to_all | solution.py:136
  78.0 46.8 %while.10 = (s32[]{:T(128)}, f32[8,256]{1,0:T(8,128)S(1)}, s32[8,256]{1,0:T(8,128)S(1)}, bf16[8,256,256]{1,2,0:T(8,128)(2,1)S(1)}, bf16[8,256]{1,0:T(8,128)(2,1)...) while((s32[]{:T(128)}, f32[8,256]{1,0:T(8,128)S(1)}, ...), condition=%wide.region_6.7_spmd, body=%wide.region_3.6_spmd.sunk | while | flops 811698688 | bytes 8822575 | solution.py:155
  78.1 0.6 fusion.383
  79.4 4.5 %conditional.2 = (f32[1,256]{1,0:T(1,128)S(1)}) conditional(s32[]{:T(128)} %bitcast.447, () %tuple.436, (s32[1,256]{1,0:T(1,128)S(1)}, bf16[8,256,256]{1,2,0:T(8,128)(2,1)S(1)}, s32[]{:T(128)}, bf16[8,256]{1,0:T(8,128)(2,1)S(1)}, bf16[3,512,128]{2,1,0:T(8,128)(2,1)S(1)}, /*index=5*/bf16[3,128,512]{2,1,0:T(8,128)(2,1)S(1)}, f32[3,512]{1,0:T(4,128)S(1)}, ...), branch_computations={%region_4.4_spmd, %region_5.5_spmd} | conditional | flops 811698688 | bytes 8818188 | solution.py:149
  79.7 0.5 fusion.4
  80.2 0.5 fusion.6
  81.2 2.3 %fusion.10 = bf16[256,512]{1,0:T(8,128)(2,1)S(1)} fusion(bf16[1024,512]{1,0:T(8,128)(2,1)} %get-tuple-element.138, bf16[256,512]{0,1:T(8,128)(2,1)S(1)} %fusion.9, bf16[512,1024]{1,0:T(8,128)(2,1)} %get-tuple-element.136, f32[1024]{0:T(1024)S(1)} %get-tuple-element.137, f32[512]{0:T(512)S(1)} %get-tuple-element.139), kind=kOutput, calls=%fused_computation.15 | convolution fusion | flops 538050560 | bytes 2627584 | tf_op jit(solution)/shard_map/while/body/eval_jaxpr/cond/branch_1_fun/dot_general | solution.py:44
  83.9 0.6 fusion.383
  85.2 4.5 %conditional.2 = (f32[1,256]{1,0:T(1,128)S(1)}) conditional(s32[]{:T(128)} %bitcast.447, () %tuple.436, (s32[1,256]{1,0:T(1,128)S(1)}, bf16[8,256,256]{1,2,0:T(8,128)(2,1)S(1)}, s32[]{:T(128)}, bf16[8,256]{1,0:T(8,128)(2,1)S(1)}, bf16[3,512,128]{2,1,0:T(8,128)(2,1)S(1)}, /*index=5*/bf16[3,128,512]{2,1,0:T(8,128)(2,1)S(1)}, f32[3,512]{1,0:T(4,128)S(1)}, ...), branch_computations={%region_4.4_spmd, %region_5.5_spmd} | conditional | flops 811698688 | bytes 8818188 | solution.py:149
  85.5 0.5 fusion.4
  86.0 0.5 fusion.6
  87.0 2.3 %fusion.10 = bf16[256,512]{1,0:T(8,128)(2,1)S(1)} fusion(bf16[1024,512]{1,0:T(8,128)(2,1)} %get-tuple-element.138, bf16[256,512]{0,1:T(8,128)(2,1)S(1)} %fusion.9, bf16[512,1024]{1,0:T(8,128)(2,1)} %get-tuple-element.136, f32[1024]{0:T(1024)S(1)} %get-tuple-element.137, f32[512]{0:T(512)S(1)} %get-tuple-element.139), kind=kOutput, calls=%fused_computation.15 | convolution fusion | flops 538050560 | bytes 2627584 | tf_op jit(solution)/shard_map/while/body/eval_jaxpr/cond/branch_1_fun/dot_general | solution.py:44
  89.7 0.6 fusion.383
  91.0 4.5 %conditional.2 = (f32[1,256]{1,0:T(1,128)S(1)}) conditional(s32[]{:T(128)} %bitcast.447, () %tuple.436, (s32[1,256]{1,0:T(1,128)S(1)}, bf16[8,256,256]{1,2,0:T(8,128)(2,1)S(1)}, s32[]{:T(128)}, bf16[8,256]{1,0:T(8,128)(2,1)S(1)}, bf16[3,512,128]{2,1,0:T(8,128)(2,1)S(1)}, /*index=5*/bf16[3,128,512]{2,1,0:T(8,128)(2,1)S(1)}, f32[3,512]{1,0:T(4,128)S(1)}, ...), branch_computations={%region_4.4_spmd, %region_5.5_spmd} | conditional | flops 811698688 | bytes 8818188 | solution.py:149
  91.4 0.5 fusion.4
  91.9 0.5 fusion.6
  92.9 2.3 %fusion.10 = bf16[256,512]{1,0:T(8,128)(2,1)S(1)} fusion(bf16[1024,512]{1,0:T(8,128)(2,1)} %get-tuple-element.138, bf16[256,512]{0,1:T(8,128)(2,1)S(1)} %fusion.9, bf16[512,1024]{1,0:T(8,128)(2,1)} %get-tuple-element.136, f32[1024]{0:T(1024)S(1)} %get-tuple-element.137, f32[512]{0:T(512)S(1)} %get-tuple-element.139), kind=kOutput, calls=%fused_computation.15 | convolution fusion | flops 538050560 | bytes 2627584 | tf_op jit(solution)/shard_map/while/body/eval_jaxpr/cond/branch_1_fun/dot_general | solution.py:44
  95.6 0.6 fusion.383
  96.9 4.5 %conditional.2 = (f32[1,256]{1,0:T(1,128)S(1)}) conditional(s32[]{:T(128)} %bitcast.447, () %tuple.436, (s32[1,256]{1,0:T(1,128)S(1)}, bf16[8,256,256]{1,2,0:T(8,128)(2,1)S(1)}, s32[]{:T(128)}, bf16[8,256]{1,0:T(8,128)(2,1)S(1)}, bf16[3,512,128]{2,1,0:T(8,128)(2,1)S(1)}, /*index=5*/bf16[3,128,512]{2,1,0:T(8,128)(2,1)S(1)}, f32[3,512]{1,0:T(4,128)S(1)}, ...), branch_computations={%region_4.4_spmd, %region_5.5_spmd} | conditional | flops 811698688 | bytes 8818188 | solution.py:149
  97.2 0.5 fusion.4
  97.7 0.5 fusion.6
  98.7 2.3 %fusion.10 = bf16[256,512]{1,0:T(8,128)(2,1)S(1)} fusion(bf16[1024,512]{1,0:T(8,128)(2,1)} %get-tuple-element.138, bf16[256,512]{0,1:T(8,128)(2,1)S(1)} %fusion.9, bf16[512,1024]{1,0:T(8,128)(2,1)} %get-tuple-element.136, f32[1024]{0:T(1024)S(1)} %get-tuple-element.137, f32[512]{0:T(512)S(1)} %get-tuple-element.139), kind=kOutput, calls=%fused_computation.15 | convolution fusion | flops 538050560 | bytes 2627584 | tf_op jit(solution)/shard_map/while/body/eval_jaxpr/cond/branch_1_fun/dot_general | solution.py:44
  101.4 0.6 fusion.383
  102.7 4.5 %conditional.2 = (f32[1,256]{1,0:T(1,128)S(1)}) conditional(s32[]{:T(128)} %bitcast.447, () %tuple.436, (s32[1,256]{1,0:T(1,128)S(1)}, bf16[8,256,256]{1,2,0:T(8,128)(2,1)S(1)}, s32[]{:T(128)}, bf16[8,256]{1,0:T(8,128)(2,1)S(1)}, bf16[3,512,128]{2,1,0:T(8,128)(2,1)S(1)}, /*index=5*/bf16[3,128,512]{2,1,0:T(8,128)(2,1)S(1)}, f32[3,512]{1,0:T(4,128)S(1)}, ...), branch_computations={%region_4.4_spmd, %region_5.5_spmd} | conditional | flops 811698688 | bytes 8818188 | solution.py:149
  103.1 0.5 fusion.4
  103.6 0.5 fusion.6
  104.6 2.3 %fusion.10 = bf16[256,512]{1,0:T(8,128)(2,1)S(1)} fusion(bf16[1024,512]{1,0:T(8,128)(2,1)} %get-tuple-element.138, bf16[256,512]{0,1:T(8,128)(2,1)S(1)} %fusion.9, bf16[512,1024]{1,0:T(8,128)(2,1)} %get-tuple-element.136, f32[1024]{0:T(1024)S(1)} %get-tuple-element.137, f32[512]{0:T(512)S(1)} %get-tuple-element.139), kind=kOutput, calls=%fused_computation.15 | convolution fusion | flops 538050560 | bytes 2627584 | tf_op jit(solution)/shard_map/while/body/eval_jaxpr/cond/branch_1_fun/dot_general | solution.py:44
  107.3 0.6 fusion.383
  108.6 4.5 %conditional.2 = (f32[1,256]{1,0:T(1,128)S(1)}) conditional(s32[]{:T(128)} %bitcast.447, () %tuple.436, (s32[1,256]{1,0:T(1,128)S(1)}, bf16[8,256,256]{1,2,0:T(8,128)(2,1)S(1)}, s32[]{:T(128)}, bf16[8,256]{1,0:T(8,128)(2,1)S(1)}, bf16[3,512,128]{2,1,0:T(8,128)(2,1)S(1)}, /*index=5*/bf16[3,128,512]{2,1,0:T(8,128)(2,1)S(1)}, f32[3,512]{1,0:T(4,128)S(1)}, ...), branch_computations={%region_4.4_spmd, %region_5.5_spmd} | conditional | flops 811698688 | bytes 8818188 | solution.py:149
  108.9 0.5 fusion.4
  109.4 0.5 fusion.6
  110.4 2.3 %fusion.10 = bf16[256,512]{1,0:T(8,128)(2,1)S(1)} fusion(bf16[1024,512]{1,0:T(8,128)(2,1)} %get-tuple-element.138, bf16[256,512]{0,1:T(8,128)(2,1)S(1)} %fusion.9, bf16[512,1024]{1,0:T(8,128)(2,1)} %get-tuple-element.136, f32[1024]{0:T(1024)S(1)} %get-tuple-element.137, f32[512]{0:T(512)S(1)} %get-tuple-element.139), kind=kOutput, calls=%fused_computation.15 | convolution fusion | flops 538050560 | bytes 2627584 | tf_op jit(solution)/shard_map/while/body/eval_jaxpr/cond/branch_1_fun/dot_general | solution.py:44
  113.1 0.6 fusion.383
  114.4 4.5 %conditional.2 = (f32[1,256]{1,0:T(1,128)S(1)}) conditional(s32[]{:T(128)} %bitcast.447, () %tuple.436, (s32[1,256]{1,0:T(1,128)S(1)}, bf16[8,256,256]{1,2,0:T(8,128)(2,1)S(1)}, s32[]{:T(128)}, bf16[8,256]{1,0:T(8,128)(2,1)S(1)}, bf16[3,512,128]{2,1,0:T(8,128)(2,1)S(1)}, /*index=5*/bf16[3,128,512]{2,1,0:T(8,128)(2,1)S(1)}, f32[3,512]{1,0:T(4,128)S(1)}, ...), branch_computations={%region_4.4_spmd, %region_5.5_spmd} | conditional | flops 811698688 | bytes 8818188 | solution.py:149
  114.8 0.5 fusion.4
  115.3 0.5 fusion.6
  116.2 2.3 %fusion.10 = bf16[256,512]{1,0:T(8,128)(2,1)S(1)} fusion(bf16[1024,512]{1,0:T(8,128)(2,1)} %get-tuple-element.138, bf16[256,512]{0,1:T(8,128)(2,1)S(1)} %fusion.9, bf16[512,1024]{1,0:T(8,128)(2,1)} %get-tuple-element.136, f32[1024]{0:T(1024)S(1)} %get-tuple-element.137, f32[512]{0:T(512)S(1)} %get-tuple-element.139), kind=kOutput, calls=%fused_computation.15 | convolution fusion | flops 538050560 | bytes 2627584 | tf_op jit(solution)/shard_map/while/body/eval_jaxpr/cond/branch_1_fun/dot_general | solution.py:44
  119.0 0.6 fusion.383
  120.3 4.5 %conditional.2 = (f32[1,256]{1,0:T(1,128)S(1)}) conditional(s32[]{:T(128)} %bitcast.447, () %tuple.436, (s32[1,256]{1,0:T(1,128)S(1)}, bf16[8,256,256]{1,2,0:T(8,128)(2,1)S(1)}, s32[]{:T(128)}, bf16[8,256]{1,0:T(8,128)(2,1)S(1)}, bf16[3,512,128]{2,1,0:T(8,128)(2,1)S(1)}, /*index=5*/bf16[3,128,512]{2,1,0:T(8,128)(2,1)S(1)}, f32[3,512]{1,0:T(4,128)S(1)}, ...), branch_computations={%region_4.4_spmd, %region_5.5_spmd} | conditional | flops 811698688 | bytes 8818188 | solution.py:149
  120.6 0.5 fusion.4
  121.1 0.5 fusion.6
  122.1 2.3 %fusion.10 = bf16[256,512]{1,0:T(8,128)(2,1)S(1)} fusion(bf16[1024,512]{1,0:T(8,128)(2,1)} %get-tuple-element.138, bf16[256,512]{0,1:T(8,128)(2,1)S(1)} %fusion.9, bf16[512,1024]{1,0:T(8,128)(2,1)} %get-tuple-element.136, f32[1024]{0:T(1024)S(1)} %get-tuple-element.137, f32[512]{0:T(512)S(1)} %get-tuple-element.139), kind=kOutput, calls=%fused_computation.15 | convolution fusion | flops 538050560 | bytes 2627584 | tf_op jit(solution)/shard_map/while/body/eval_jaxpr/cond/branch_1_fun/dot_general | solution.py:44
  124.8 0.6 reshape_reshape.3
  (428 shorter events, 33.6 us)
Async XLA Ops:
  0.0 28.9 %copy-start.4 = (bf16[8,128,256]{2,1,0:T(8,128)(2,1)S(1)}, bf16[8,128,256]{2,1,0:T(8,128)(2,1)}, u32[]{:S(2)}) copy-start(bf16[8,128,256]{2,1,0:T(8,128)(2,1)} %param.21) | copy-start | bytes 1572868
  50.6 18.4 %copy-start.2 = (bf16[1,1,2048,256]{3,2,1,0:T(8,128)(2,1)S(1)}, bf16[1,1,2048,256]{3,2,1,0:T(8,128)(2,1)}, u32[]{:S(2)}) copy-start(bf16[1,1,2048,256]{3,2,1,0:T(8,128)(2,1)} %param.24) | copy-start | bytes 3145732
  54.3 15.2 %copy-start.9 = (s32[1,1,8]{2,1,0:T(1,128)S(1)}, s32[1,1,8]{2,1,0:T(1,128)}, u32[]{:S(2)}) copy-start(s32[1,1,8]{2,1,0:T(1,128)} %param.25) | copy-start | bytes 100
  54.3 23.7 %copy-start = (bf16[3,512,128]{2,1,0:T(8,128)(2,1)S(1)}, bf16[3,512,128]{2,1,0:T(8,128)(2,1)}, u32[]{:S(2)}) copy-start(bf16[3,512,128]{2,1,0:T(8,128)(2,1)} %param.26) | copy-start | bytes 1179652
  54.3 23.7 %copy-start.1 = (bf16[3,128,512]{2,1,0:T(8,128)(2,1)S(1)}, bf16[3,128,512]{2,1,0:T(8,128)(2,1)}, u32[]{:S(2)}) copy-start(bf16[3,128,512]{2,1,0:T(8,128)(2,1)} %param.27) | copy-start | bytes 1179652
  54.3 23.7 %copy-start.3 = (f32[3,512]{1,0:T(4,128)S(1)}, f32[3,512]{1,0:T(4,128)}, u32[]{:S(2)}) copy-start(f32[3,512]{1,0:T(4,128)} %param.28) | copy-start | bytes 18436
  54.3 23.7 %copy-start.5 = (bf16[512,256]{1,0:T(8,128)(2,1)S(1)}, bf16[512,256]{1,0:T(8,128)(2,1)}, u32[]{:S(2)}) copy-start(bf16[512,256]{1,0:T(8,128)(2,1)} %param.33) | copy-start | bytes 786436
  54.3 23.7 %copy-start.6 = (f32[1024]{0:T(1024)S(1)}, f32[1024]{0:T(1024)}, u32[]{:S(2)}) copy-start(f32[1024]{0:T(1024)} %param.30) | copy-start | bytes 12292
  54.3 23.7 %copy-start.7 = (f32[512]{0:T(512)S(1)}, f32[512]{0:T(512)}, u32[]{:S(2)}) copy-start(f32[512]{0:T(512)} %param.32) | copy-start | bytes 6148
  54.4 23.7 %copy-start.8 = (f32[256]{0:T(256)S(1)}, f32[256]{0:T(256)}, u32[]{:S(2)}) copy-start(f32[256]{0:T(256)} %param.34) | copy-start | bytes 3076
  54.4 23.6 %copy-start.10 = (bf16[256]{0:T(256)(128)(2,1)S(1)}, bf16[256]{0:T(256)(128)(2,1)}, u32[]{:S(2)}) copy-start(bf16[256]{0:T(256)(128)(2,1)} %param.35) | copy-start | bytes 1540
  63.1 14.8 %all-to-all-start = ((bf16[8,8,1,8,256]{4,3,1,2,0:T(8,128)(2,1)}), bf16[8,8,1,8,256]{4,3,1,2,0:T(8,128)(2,1)S(1)}, u32[]{:S(2)}, u32[]{:S(2)}) async-start(bf16[8,8,1,8,256]{4,3,1,2,0:T(8,128)(2,1)} %constant_dynamic-update-slice_fusion), calls=%async_computation | async-start | bytes 524288 | tf_op jit(solution)/shard_map/all_to_all | solution.py:136
